TPU v7x, 256 devices: a whole 4x4x8 slice. The times are simulated.
256 devices in a mesh: seq: 16 (over y, z_hi), fsdp: 16 (over x, z_lo, core).
Axes of the slice: x: 4, y: 4, z: 8 (z_hi: 4, z_lo: 2; z = z_hi * 2 + z_lo), core: 2. Of those that a mesh axis runs over, the one named last changes fastest.
Arguments:
- tokens: bfloat16 [2048, 4096], P('seq', 'fsdp'), may hold values from -6 to 6
- in_weight: bfloat16 [3, 4096, 4096], P(None, 'seq', 'fsdp'), may hold values from -0.09375 to 0.09375
- out_weight: bfloat16 [4096, 4096], P('fsdp', 'seq'), may hold values from -0.09375 to 0.09375
- filters: float32 [4096, 128], P('fsdp'), may hold values from -0.5 to 0.5
- cotangent: bfloat16 [2048, 4096], P('seq', 'fsdp'), may hold values from -6 to 6
Outputs:
- mixed_out: bfloat16 [2048, 4096], P('seq', 'fsdp')
- grad_tokens: bfloat16 [2048, 4096], P('seq', 'fsdp')
- grad_in_weight: float32 [3, 4096, 4096], P(None, 'seq', 'fsdp')
- grad_out_weight: float32 [4096, 4096], P('fsdp', 'seq')
- grad_filters: float32 [4096, 128], P('fsdp')
All inputs are finite; a program needn't handle non-finite values.
Results may differ from a plain program's by a relative error of at most 0.018.
Values may be sent and summed in bfloat16 or wider, within the bound.
A program may use at most 64 MiB of HBM per device.

v0:
```python
import jax
import jax.numpy as jnp
from jax import lax
from jax.sharding import PartitionSpec as P

highest = lax.Precision.HIGHEST


def from_behind(value, axis, by):
    length = lax.axis_size(axis)
    pairs = [(i, i + by) for i in range(length) if 0 <= i + by < length]
    return lax.ppermute(value, axis, pairs)


def causal_filter(extended, filters):
    kernel = jnp.flip(jnp.transpose(filters), 0)[:, None, :]
    result = lax.conv_general_dilated(
        extended[None],
        kernel,
        (1,),
        "VALID",
        dimension_numbers=("NWC", "WIO", "NWC"),
        feature_group_count=filters.shape[0],
        precision=highest,
    )
    return result[0]


def reverse_filter(extended, filters):
    kernel = jnp.transpose(filters)[:, None, :]
    result = lax.conv_general_dilated(
        extended[None],
        kernel,
        (1,),
        "VALID",
        dimension_numbers=("NWC", "WIO", "NWC"),
        feature_group_count=filters.shape[0],
        precision=highest,
    )
    return result[0]


def filter_grad(extended, gradient):
    result = lax.conv_general_dilated(
        extended[None],
        gradient[:, None, :],
        (1,),
        "VALID",
        dimension_numbers=("NWC", "WIO", "NWC"),
        feature_group_count=gradient.shape[1],
        precision=highest,
    )
    return jnp.transpose(jnp.flip(result[0], 0))


def on_device(tokens, in_weight, out_weight, filters, cotangent):
    margin = filters.shape[1] - 1
    gathered = lax.all_gather(tokens, "fsdp", axis=1, tiled=True)
    out_full = lax.all_gather(out_weight, "seq", axis=1, tiled=True)
    in_full = lax.all_gather(in_weight, "seq", axis=1, tiled=True)
    projected = jnp.einsum("td,idc->itc", gathered, in_full, preferred_element_type=jnp.float32)
    projected = projected.astype(jnp.bfloat16)
    queries = projected[0].astype(jnp.float32)
    key_part = projected[1].astype(jnp.float32)
    value_part = projected[2].astype(jnp.float32)
    signal = (key_part * value_part).astype(jnp.bfloat16)
    earlier = from_behind(signal[-margin:], "seq", 1)
    extended = jnp.concatenate([earlier, signal], 0).astype(jnp.float32)
    filtered = causal_filter(extended, filters)
    gated_rows = (queries * filtered).astype(jnp.bfloat16)
    partial_value = jnp.dot(gated_rows, out_full, preferred_element_type=jnp.float32)
    mixed_out = lax.psum_scatter(
        partial_value.astype(jnp.bfloat16), "fsdp", scatter_dimension=1, tiled=True
    )
    grad_full = lax.all_gather(cotangent, "fsdp", axis=1, tiled=True)
    grad_gated = lax.dot_general(
        grad_full, out_full, (((1,), (1,)), ((), ())), preferred_element_type=jnp.float32
    )
    grad_queries = grad_gated * filtered
    grad_filtered = (grad_gated * queries).astype(jnp.bfloat16)
    later_rows = from_behind(grad_filtered[:margin], "seq", -1)
    grad_signal = reverse_filter(
        jnp.concatenate([grad_filtered, later_rows], 0).astype(jnp.float32), filters
    )
    grad_filters = lax.psum(
        filter_grad(extended, grad_filtered.astype(jnp.float32)).astype(jnp.bfloat16), "seq"
    ).astype(jnp.float32)
    grad_projected = jnp.stack(
        [grad_queries, grad_signal * value_part, grad_signal * key_part]
    ).astype(jnp.bfloat16)
    grad_partial = jnp.einsum(
        "itc,idc->td", grad_projected, in_full, preferred_element_type=jnp.float32
    )
    grad_tokens = lax.psum_scatter(
        grad_partial.astype(jnp.bfloat16), "fsdp", scatter_dimension=1, tiled=True
    )
    weight_in_part = jnp.einsum(
        "td,itc->idc", gathered, grad_projected, preferred_element_type=jnp.float32
    )
    weight_out_part = lax.dot_general(
        gated_rows, grad_full, (((0,), (0,)), ((), ())), preferred_element_type=jnp.float32
    )
    grad_in_weight, grad_out_weight = (
        lax.psum_scatter(
            weight_in_part.astype(jnp.bfloat16), "seq", scatter_dimension=1, tiled=True
        ).astype(jnp.float32),
        lax.psum_scatter(
            weight_out_part.astype(jnp.bfloat16), "seq", scatter_dimension=1, tiled=True
        ).astype(jnp.float32),
    )
    return (mixed_out, grad_tokens, grad_in_weight, grad_out_weight, grad_filters)


def solution(mesh):
    placed = (
        P("seq", "fsdp"),
        P(None, "seq", "fsdp"),
        P("fsdp", "seq"),
        P("fsdp", None),
        P("seq", "fsdp"),
    )
    return jax.shard_map(
        on_device,
        mesh=mesh,
        in_specs=placed,
        out_specs=(
            P("seq", "fsdp"),
            P("seq", "fsdp"),
            P(None, "seq", "fsdp"),
            P("fsdp", "seq"),
            P("fsdp", None),
        ),
        check_vma=False,
    )
```

profile of v0, /device:TPU:16, one launch (start us, length us, event | category | flops | bytes accessed | tf_op | source)
XLA Modules:
  0.0 766.9 jit_solution(3096591360201777987)
XLA Ops:
  7.2 0.0 all-gather.7.cloned.1.call-start
  7.2 0.7 all-gather.7.cloned.1.call-update
  7.9 0.0 all-gather.5.cloned.1.call-start
  7.9 0.7 all-gather.5.cloned.1.call-update
  8.6 0.0 all-gather.11.cloned.1.call-start
  8.7 0.7 all-gather.11.cloned.1.call-update
  9.4 0.0 all-gather.9.cloned.1.call-start
  9.4 0.5 all-gather.9.cloned.1.call-update
  10.0 0.0 copy-start.3
  10.0 0.0 all-reduce.2.cloned.1.call-start
  10.0 38.7 %all-gather.7.cloned.1.call-done = bf16[128,4096]{1,0:T(8,128)(2,1)} async-done(((bf16[128,256]{1,0:T(8,128)(2,1)}), bf16[128,4096]{1,0:T(8,128)(2,1)}) %all-gather.7.cloned.1.call-update) | async-done | bytes 1048592 | tf_op jit(solution)/shard_map/all_gather | solution.py:58
  48.7 93.1 %all-gather.5.cloned.1.call-done = bf16[3,4096,256]{2,1,0:T(8,128)(2,1)} async-done(((bf16[3,256,256]{2,1,0:T(8,128)(2,1)}), bf16[3,4096,256]{2,1,0:T(8,128)(2,1)}) %all-gather.5.cloned.1.call-update) | async-done | bytes 6291472 | tf_op jit(solution)/shard_map/all_gather | solution.py:60
  141.8 4.1 fusion.2
  145.9 38.9 %all-gather.11.cloned.1.call-done = bf16[128,4096]{1,0:T(8,128)(2,1)} async-done(((bf16[128,256]{1,0:T(8,128)(2,1)}), bf16[128,4096]{1,0:T(8,128)(2,1)}) %all-gather.11.cloned.1.call-update) | async-done | bytes 1048592 | tf_op jit(solution)/shard_map/all_gather | solution.py:75
  184.8 64.7 %all-gather.9.cloned.1.call-done = bf16[256,4096]{1,0:T(8,128)(2,1)} async-done(((bf16[256,256]{1,0:T(8,128)(2,1)}), bf16[256,4096]{1,0:T(8,128)(2,1)}) %all-gather.9.cloned.1.call-update) | async-done | bytes 2097168 | tf_op jit(solution)/shard_map/all_gather | solution.py:59
  249.5 2.8 fusion.15
  252.3 3.5 collective-permute-start.1
  255.8 0.1 copy.13
  255.9 3.4 collective-permute-done.1
  259.4 1.4 fusion.5
  260.8 3.8 collective-permute-start
  264.7 0.2 rev.7
  264.9 0.1 copy.11
  265.0 5.0 collective-permute-done
  270.0 1.4 fusion.9
  271.5 1.9 fusion.7
  273.4 0.7 rev.8
  274.0 0.0 all-reduce.2.cloned.1.call-update
  274.1 0.0 reduce-scatter.11.cloned.1.call-start
  274.1 2.0 convolution_convert_fusion.1
  276.2 0.0 reduce-scatter.11.cloned.1.call-update
  276.2 0.0 reduce-scatter.9.cloned.1.call-start
  276.3 4.4 fusion
  280.7 0.0 reduce-scatter.9.cloned.1.call-update
  280.8 0.0 reduce-scatter.7.cloned.1.call-start
  280.8 6.0 fusion.1
  286.8 0.0 reduce-scatter.7.cloned.1.call-update
  286.9 0.0 reduce-scatter.5.cloned.1.call-start
  286.9 1.5 convolution_convert_fusion.2
  288.4 0.0 reduce-scatter.5.cloned.1.call-update
  288.4 137.5 %all-reduce.2.cloned.1.call-done = bf16[256,128]{0,1:T(8,128)(2,1)} async-done(((bf16[256,128]{0,1:T(8,128)(2,1)}), bf16[256,128]{0,1:T(8,128)(2,1)}) %all-reduce.2.cloned.1.call-update) | async-done | bytes 65552 | tf_op jit(solution)/shard_map/psum | solution.py:85
  425.9 1.6 copy.20
  427.5 87.5 %reduce-scatter.11.cloned.1.call-done = bf16[256,256]{1,0:T(8,128)(2,1)} async-done(((bf16[256,4096]{1,0:T(8,128)(2,1)}), bf16[256,256]{1,0:T(8,128)(2,1)}) %reduce-scatter.11.cloned.1.call-update) | async-done | bytes 131088 | tf_op jit(solution)/shard_map/reduce_scatter | solution.py:107
  515.1 1.6 convert_element_type.84
  516.7 110.3 %reduce-scatter.9.cloned.1.call-done = bf16[3,256,256]{1,2,0:T(8,128)(2,1)} async-done(((bf16[3,4096,256]{1,2,0:T(8,128)(2,1)}), bf16[3,256,256]{1,2,0:T(8,128)(2,1)}) %reduce-scatter.9.cloned.1.call-update) | async-done | bytes 393232 | tf_op jit(solution)/shard_map/reduce_scatter | solution.py:104
  627.0 2.0 copy.19
  629.0 65.3 %reduce-scatter.7.cloned.1.call-done = bf16[128,256]{1,0:T(8,128)(2,1)} async-done(((bf16[128,4096]{1,0:T(8,128)(2,1)}), bf16[128,256]{1,0:T(8,128)(2,1)}) %reduce-scatter.7.cloned.1.call-update) | async-done | bytes 65552 | tf_op jit(solution)/shard_map/reduce_scatter | solution.py:94
  694.3 66.1 %reduce-scatter.5.cloned.1.call-done = bf16[128,256]{1,0:T(8,128)(2,1)} async-done(((bf16[128,4096]{1,0:T(8,128)(2,1)}), bf16[128,256]{1,0:T(8,128)(2,1)}) %reduce-scatter.5.cloned.1.call-update) | async-done | bytes 65552 | tf_op jit(solution)/shard_map/reduce_scatter | solution.py:72
  (13 shorter events, 0.1 us)
Async XLA Ops:
  7.2 41.6 %all-gather.7.cloned.1.call-start = ((), (), s32[]{:S(2)}) async-start(), calls=%async_computation.5 | async-start | bytes 1114112 | tf_op jit(solution)/shard_map/all_gather | solution.py:58
  7.9 133.9 %all-gather.5.cloned.1.call-start = ((), (), s32[]{:S(2)}) async-start(), calls=%async_computation.4 | async-start | bytes 6684672 | tf_op jit(solution)/shard_map/all_gather | solution.py:60
  8.6 176.2 %all-gather.11.cloned.1.call-start = ((), (), s32[]{:S(2)}) async-start(), calls=%async_computation.8 | async-start | bytes 1114112 | tf_op jit(solution)/shard_map/all_gather | solution.py:75
  9.4 240.1 %all-gather.9.cloned.1.call-start = ((), (), s32[]{:S(2)}) async-start(), calls=%async_computation.6 | async-start | bytes 2228224 | tf_op jit(solution)/shard_map/all_gather | solution.py:59
  10.0 245.8 %copy-start.3 = (f32[256,128]{1,0:T(8,128)S(1)}, f32[256,128]{1,0:T(8,128)}, u32[]{:S(2)}) copy-start(f32[256,128]{1,0:T(8,128)} %param.8) | copy-start | bytes 393220
  10.0 416.0 %all-reduce.2.cloned.1.call-start = ((), (), s32[]{:S(2)}) async-start(), calls=%async_computation.12 | async-start | bytes 131072 | tf_op jit(solution)/shard_map/psum | solution.py:85
  252.3 7.1 collective-permute-start.1
  260.8 9.2 %collective-permute-start = (bf16[127,256]{1,0:T(8,128)(2,1)S(1)}, bf16[127,256]{1,0:T(8,128)(2,1)S(1)}, u32[]{:S(2)}, u32[]{:S(2)}) collective-permute-start(bf16[127,256]{1,0:T(8,128)(2,1)S(1)} %slice_bitcast_fusion), channel_id=1, source_target_pairs={{0,16},{16,32},{32,48},{48,64},{64,80},{80,96},{96,112},{112,128},... | collective-permute-start | bytes 195080 | tf_op jit(solution)/shard_map/ppermute | solution.py:12
  271.4 2.7 copy-start.2
  273.3 2.9 copy-start.1
  274.1 241.0 %reduce-scatter.11.cloned.1.call-start = ((), (), s32[]{:S(2)}) async-start(), calls=%async_computation.11 | async-start | bytes 2228224 | tf_op jit(solution)/shard_map/reduce_scatter | solution.py:107
  276.2 350.8 %reduce-scatter.9.cloned.1.call-start = ((), (), s32[]{:S(2)}) async-start(), calls=%async_computation.10 | async-start | bytes 6684672 | tf_op jit(solution)/shard_map/reduce_scatter | solution.py:104
  280.7 6.2 copy-start
  280.8 413.5 %reduce-scatter.7.cloned.1.call-start = ((), (), s32[]{:S(2)}) async-start(), calls=%async_computation.9 | async-start | bytes 1114112 | tf_op jit(solution)/shard_map/reduce_scatter | solution.py:94
  286.9 473.5 %reduce-scatter.5.cloned.1.call-start = ((), (), s32[]{:S(2)}) async-start(), calls=%async_computation.7 | async-start | bytes 1114112 | tf_op jit(solution)/shard_map/reduce_scatter | solution.py:72
Sparse Core Ops, SparseCore 0:
  9.7 38.9 all-gather.6
  51.2 90.5 all-gather.4
  143.6 41.1 all-gather.10
  187.1 62.4 all-gather.8
  274.2 151.6 all-reduce.1
  429.3 85.6 reduce-scatter.10
  518.8 108.1 reduce-scatter.8
  630.0 64.1 reduce-scatter.6
  697.4 62.9 reduce-scatter.4
where the time goes:
time: 767 us
  waiting for transfers between devices  713 us (93%)
  matrix products  25.5 us (3%)
  between operations  14 us (2%)
  starting transfers between devices  7.7 us (1%)
    psum x1, waiting for transfers between devices, on_device(): lax.psum(filter_grad(extended, grad_filtered.astype(jnp.float32)).astype(...  138 us
    reduce_scatter x1, waiting for transfers between devices, on_device(): lax.psum_scatter(weight_in_part.astype(jnp.bfloat16), 'seq', scatter_dime...  110 us
    all_gather x1, waiting for transfers between devices, on_device(): in_full = lax.all_gather(in_weight, 'seq', axis=1, tiled=True)  93.1 us
    reduce_scatter x1, waiting for transfers between devices, on_device(): lax.psum_scatter(weight_out_part.astype(jnp.bfloat16), 'seq', scatter_dim...  87.5 us
    reduce_scatter x1, waiting for transfers between devices, on_device(): lax.psum_scatter(partial_value.astype(jnp.bfloat16), 'fsdp', scatter_dime...  66.1 us
    reduce_scatter x1, waiting for transfers between devices, on_device(): lax.psum_scatter(grad_partial.astype(jnp.bfloat16), 'fsdp', scatter_dimen...  65.3 us
    all_gather x1, waiting for transfers between devices, on_device(): out_full = lax.all_gather(out_weight, 'seq', axis=1, tiled=True)  64.7 us
    all_gather x1, waiting for transfers between devices, on_device(): grad_full = lax.all_gather(cotangent, 'fsdp', axis=1, tiled=True)  38.9 us
  transfers between devices with their start and end apart: 11, of which 11 were waited for; matrix products, arithmetic and copies ran while one was open for 3% of the time, Pallas kernels for 0%

commit v1 on v0

--- a/solution.py
+++ b/solution.py
@@ -56,7 +56,9 @@
 def on_device(tokens, in_weight, out_weight, filters, cotangent):
     margin = filters.shape[1] - 1
     gathered = lax.all_gather(tokens, "fsdp", axis=1, tiled=True)
-    out_full = lax.all_gather(out_weight, "seq", axis=1, tiled=True)
+    out_full = jnp.concatenate(
+        lax.all_to_all(jnp.stack([out_weight] * lax.axis_size("seq")), "seq", 0, 0), axis=1
+    )
     in_full = lax.all_gather(in_weight, "seq", axis=1, tiled=True)
     projected = jnp.einsum("td,idc->itc", gathered, in_full, preferred_element_type=jnp.float32)
     projected = projected.astype(jnp.bfloat16)

time: 767 us -> 722 us (0.941)
  waiting for transfers between devices: 713 us -> 646 us
  starting transfers between devices: 7.7 us -> 22.7 us
    all_gather x1 -> x0, waiting for transfers between devices: 64.7 us -> none  [on_device(): out_full = lax.all_gather(out_weight, 'seq', axis=1, tiled=True)]
    all_to_all x0 -> x1, starting transfers between devices: none -> 11.4 us  [on_device(): lax.all_to_all(jnp.stack([out_weight] * lax.axis_size('seq')), 'seq', 0, 0)]
  transfers between devices with their start and end apart: 11 -> 11, of which waited for: 11 -> 10; matrix products, arithmetic and copies ran while one was open for 3% -> 4% of each run, Pallas kernels for 0% -> 0%
where the time goes in v1:
time: 722 us
  waiting for transfers between devices  646 us (89%)
  matrix products  27.5 us (4%)
  starting transfers between devices  22.7 us (3%)
  between operations  14.3 us (2%)
  local copies, waits for them, and re-layouts  8 us (1%)
    psum x1, waiting for transfers between devices, on_device(): lax.psum(filter_grad(extended, grad_filtered.astype(jnp.float32)).astype(...  135 us
    reduce_scatter x1, waiting for transfers between devices, on_device(): lax.psum_scatter(weight_in_part.astype(jnp.bfloat16), 'seq', scatter_dime...  110 us
    all_gather x1, waiting for transfers between devices, on_device(): in_full = lax.all_gather(in_weight, 'seq', axis=1, tiled=True)  96.3 us
    reduce_scatter x1, waiting for transfers between devices, on_device(): lax.psum_scatter(weight_out_part.astype(jnp.bfloat16), 'seq', scatter_dim...  87.7 us
    reduce_scatter x1, waiting for transfers between devices, on_device(): lax.psum_scatter(grad_partial.astype(jnp.bfloat16), 'fsdp', scatter_dimen...  65.9 us
    reduce_scatter x1, waiting for transfers between devices, on_device(): lax.psum_scatter(partial_value.astype(jnp.bfloat16), 'fsdp', scatter_dime...  65.1 us
    all_gather x1, waiting for transfers between devices, on_device(): grad_full = lax.all_gather(cotangent, 'fsdp', axis=1, tiled=True)  38.9 us
    all_gather x1, waiting for transfers between devices, on_device(): gathered = lax.all_gather(tokens, 'fsdp', axis=1, tiled=True)  37.4 us
  transfers between devices with their start and end apart: 11, of which 10 were waited for; matrix products, arithmetic and copies ran while one was open for 4% of the time, Pallas kernels for 0%

profile of v1, /device:TPU:16, one launch (start us, length us, event | category | flops | bytes accessed | tf_op | source)
XLA Modules:
  0.0 721.6 jit_solution(14588080221168039738)
XLA Ops:
  7.2 0.0 all-gather.6.cloned.1.call-start
  7.2 0.7 all-gather.6.cloned.1.call-update
  7.9 0.0 all-gather.4.cloned.1.call-start
  7.9 0.7 all-gather.4.cloned.1.call-update
  8.6 1.0 copy.25
  9.7 1.6 stack.8
  11.2 11.4 %all-to-all-start = ((bf16[16,256,256]{1,2,0:T(8,128)(2,1)}), bf16[16,256,256]{1,2,0:T(8,128)(2,1)S(1)}, u32[]{:S(2)}, u32[]{:S(2)}) async-start(bf16[16,256,256]{1,2,0:T(8,128)(2,1)} %stack.8), calls=%async_computation | async-start | bytes 4194304 | tf_op jit(solution)/shard_map/all_to_all | solution.py:60
  22.7 0.0 all-gather.8.cloned.1.call-start
  22.7 0.7 all-gather.8.cloned.1.call-update
  23.4 0.0 all-reduce.2.cloned.1.call-start
  23.4 37.4 %all-gather.6.cloned.1.call-done = bf16[128,4096]{1,0:T(8,128)(2,1)} async-done(((bf16[128,256]{1,0:T(8,128)(2,1)}), bf16[128,4096]{1,0:T(8,128)(2,1)}) %all-gather.6.cloned.1.call-update) | async-done | bytes 1048592 | tf_op jit(solution)/shard_map/all_gather | solution.py:58
  60.9 96.3 %all-gather.4.cloned.1.call-done = bf16[3,4096,256]{2,1,0:T(8,128)(2,1)} async-done(((bf16[3,256,256]{2,1,0:T(8,128)(2,1)}), bf16[3,4096,256]{2,1,0:T(8,128)(2,1)}) %all-gather.4.cloned.1.call-update) | async-done | bytes 6291472 | tf_op jit(solution)/shard_map/all_gather | solution.py:62
  157.1 4.1 fusion.2
  161.3 38.9 %all-gather.8.cloned.1.call-done = bf16[128,4096]{1,0:T(8,128)(2,1)} async-done(((bf16[128,256]{1,0:T(8,128)(2,1)}), bf16[128,4096]{1,0:T(8,128)(2,1)}) %all-gather.8.cloned.1.call-update) | async-done | bytes 1048592 | tf_op jit(solution)/shard_map/all_gather | solution.py:77
  200.1 2.3 fusion.13
  202.5 5.7 collective-permute-start.1
  208.2 0.1 copy.27
  208.4 3.0 collective-permute-done.1
  211.4 1.4 fusion.5
  212.8 0.7 fusion.18
  213.5 5.2 collective-permute-start
  218.7 0.2 rev.7
  218.9 0.1 copy.23
  219.0 4.1 collective-permute-done
  223.1 1.4 fusion.9
  224.5 1.9 fusion.7
  226.4 0.7 rev.8
  227.1 0.0 all-reduce.2.cloned.1.call-update
  227.2 0.0 reduce-scatter.11.cloned.1.call-start
  227.2 3.4 convolution_convert_fusion.1
  230.6 0.0 reduce-scatter.11.cloned.1.call-update
  230.6 0.0 reduce-scatter.9.cloned.1.call-start
  230.7 0.9 fusion.21
  231.6 0.6 copy-done.2
  232.2 5.3 fusion
  237.5 0.0 reduce-scatter.9.cloned.1.call-update
  237.5 0.0 reduce-scatter.5.cloned.1.call-start
  237.6 1.8 convolution_convert_fusion.2
  239.4 0.0 reduce-scatter.7.cloned.1.call-start
  239.5 5.9 fusion.1
  245.4 135.0 %all-reduce.2.cloned.1.call-done = bf16[256,128]{0,1:T(8,128)(2,1)} async-done(((bf16[256,128]{0,1:T(8,128)(2,1)}), bf16[256,128]{0,1:T(8,128)(2,1)}) %all-reduce.2.cloned.1.call-update) | async-done | bytes 65552 | tf_op jit(solution)/shard_map/psum | solution.py:87
  380.4 1.6 copy.34
  382.0 87.7 %reduce-scatter.11.cloned.1.call-done = bf16[256,256]{1,0:T(8,128)(2,1)} async-done(((bf16[256,4096]{1,0:T(8,128)(2,1)}), bf16[256,256]{1,0:T(8,128)(2,1)}) %reduce-scatter.11.cloned.1.call-update) | async-done | bytes 131088 | tf_op jit(solution)/shard_map/reduce_scatter | solution.py:109
  469.7 1.6 convert_element_type.95
  471.3 110.4 %reduce-scatter.9.cloned.1.call-done = bf16[3,256,256]{1,2,0:T(8,128)(2,1)} async-done(((bf16[3,4096,256]{1,2,0:T(8,128)(2,1)}), bf16[3,256,256]{1,2,0:T(8,128)(2,1)}) %reduce-scatter.9.cloned.1.call-update) | async-done | bytes 393232 | tf_op jit(solution)/shard_map/reduce_scatter | solution.py:106
  581.7 2.0 copy.33
  583.8 65.1 %reduce-scatter.5.cloned.1.call-done = bf16[128,256]{1,0:T(8,128)(2,1)} async-done(((bf16[128,4096]{1,0:T(8,128)(2,1)}), bf16[128,256]{1,0:T(8,128)(2,1)}) %reduce-scatter.5.cloned.1.call-update) | async-done | bytes 65552 | tf_op jit(solution)/shard_map/reduce_scatter | solution.py:74
  648.9 65.9 %reduce-scatter.7.cloned.1.call-done = bf16[128,256]{1,0:T(8,128)(2,1)} async-done(((bf16[128,4096]{1,0:T(8,128)(2,1)}), bf16[128,256]{1,0:T(8,128)(2,1)}) %reduce-scatter.7.cloned.1.call-update) | async-done | bytes 65552 | tf_op jit(solution)/shard_map/reduce_scatter | solution.py:96
  (16 shorter events, 0.1 us)
Async XLA Ops:
  7.2 53.7 %all-gather.6.cloned.1.call-start = ((), (), s32[]{:S(2)}) async-start(), calls=%async_computation.6 | async-start | bytes 1114112 | tf_op jit(solution)/shard_map/all_gather | solution.py:58
  7.9 149.2 %all-gather.4.cloned.1.call-start = ((), (), s32[]{:S(2)}) async-start(), calls=%async_computation.5 | async-start | bytes 6684672 | tf_op jit(solution)/shard_map/all_gather | solution.py:62
  11.2 188.9 %all-to-all-start = ((bf16[16,256,256]{1,2,0:T(8,128)(2,1)}), bf16[16,256,256]{1,2,0:T(8,128)(2,1)S(1)}, u32[]{:S(2)}, u32[]{:S(2)}) async-start(bf16[16,256,256]{1,2,0:T(8,128)(2,1)} %stack.8), calls=%async_computation | async-start | bytes 4194304 | tf_op jit(solution)/shard_map/all_to_all | solution.py:60
  22.7 177.5 %all-gather.8.cloned.1.call-start = ((), (), s32[]{:S(2)}) async-start(), calls=%async_computation.8 | async-start | bytes 1114112 | tf_op jit(solution)/shard_map/all_gather | solution.py:77
  23.4 357.0 %all-reduce.2.cloned.1.call-start = ((), (), s32[]{:S(2)}) async-start(), calls=%async_computation.12 | async-start | bytes 131072 | tf_op jit(solution)/shard_map/psum | solution.py:87
  161.2 47.0 %copy-start.4 = (f32[256,128]{1,0:T(8,128)S(1)}, f32[256,128]{1,0:T(8,128)}, u32[]{:S(2)}) copy-start(f32[256,128]{1,0:T(8,128)} %param.8) | copy-start | bytes 393220
  202.5 8.9 %collective-permute-start.1 = (bf16[127,256]{1,0:T(8,128)(2,1)S(1)}, bf16[127,256]{1,0:T(8,128)(2,1)S(1)}, u32[]{:S(2)}, u32[]{:S(2)}) collective-permute-start(bf16[127,256]{1,0:T(8,128)(2,1)S(1)} %bitcast.75), channel_id=1, source_target_pairs={{16,0},{32,16},{48,32},{64,48},{80,64},{96,80},{112,96},{128,112},... | collective-permute-start | bytes 195080 | tf_op jit(solution)/shard_map/ppermute | solution.py:12
  213.5 9.6 %collective-permute-start = (bf16[127,256]{1,0:T(8,128)(2,1)S(1)}, bf16[127,256]{1,0:T(8,128)(2,1)S(1)}, u32[]{:S(2)}, u32[]{:S(2)}) collective-permute-start(bf16[127,256]{1,0:T(8,128)(2,1)S(1)} %slice_bitcast_fusion), channel_id=1, source_target_pairs={{0,16},{16,32},{32,48},{48,64},{64,80},{80,96},{96,112},{112,128},... | collective-permute-start | bytes 195080 | tf_op jit(solution)/shard_map/ppermute | solution.py:12
  227.1 5.1 copy-start
  227.2 242.5 %reduce-scatter.11.cloned.1.call-start = ((), (), s32[]{:S(2)}) async-start(), calls=%async_computation.11 | async-start | bytes 2228224 | tf_op jit(solution)/shard_map/reduce_scatter | solution.py:109
  230.6 351.1 %reduce-scatter.9.cloned.1.call-start = ((), (), s32[]{:S(2)}) async-start(), calls=%async_computation.10 | async-start | bytes 6684672 | tf_op jit(solution)/shard_map/reduce_scatter | solution.py:106
  231.6 0.6 copy-start.2
  237.5 2.0 copy-start.1
  237.5 2.0 copy-start.3
  237.5 411.3 %reduce-scatter.5.cloned.1.call-start = ((), (), s32[]{:S(2)}) async-start(), calls=%async_computation.7 | async-start | bytes 1114112 | tf_op jit(solution)/shard_map/reduce_scatter | solution.py:74
  239.4 475.3 %reduce-scatter.7.cloned.1.call-start = ((), (), s32[]{:S(2)}) async-start(), calls=%async_computation.9 | async-start | bytes 1114112 | tf_op jit(solution)/shard_map/reduce_scatter | solution.py:96
Sparse Core Ops, SparseCore 0:
  9.7 51.0 all-gather.5
  63.4 93.7 all-gather.3
  158.9 41.1 all-gather.7
  227.3 153.0 all-reduce.1
  383.8 85.8 reduce-scatter.10
  473.3 108.4 reduce-scatter.8
  584.8 64.0 reduce-scatter.4
  652.0 62.7 reduce-scatter.6
